TPU v7x, 32 devices: a whole 2x2x4 slice. The times are simulated.
32 devices in a mesh: group: 2 (over y), col: 4 (over z), row: 2 (over x), section: 2 (over core).
Axes of the slice: x: 2, y: 2, z: 4, core: 2. Of those that a mesh axis runs over, the one named last changes fastest.
Arguments:
- tokens: bfloat16 [2, 256, 8192], P(None, ('group', 'col'), 'row'), parts along dimension 1, may hold values from -12 to 12, as said below
- norm_gain: float32 [2, 8192], P('section', 'row'), may hold values from 0.5 to 1.5
- w_gate: bfloat16 [2, 8192, 14336], P('section', 'row', 'col'), may hold values from -0.0625 to 0.0625
- w_up: bfloat16 [2, 8192, 14336], P('section', 'row', 'col'), may hold values from -0.0625 to 0.0625
- w_down: bfloat16 [2, 14336, 8192], P('section', 'col', 'row'), may hold values from -0.046875 to 0.046875
Outputs:
- block_out: bfloat16 [2, 2, 256, 8192], P('section', None, ('group', 'col'), 'row'), parts along dimension 2
There are 2 independent parts, one for each index of `group`. A program takes and returns all parts, laid end to end along the dimension named above; an argument that names none is the same for every part. Nothing has to cross between parts.
Inputs may be any that keep to these rules, and one draw needn't show every extreme that they name: `tokens`: dense real activations.
All inputs are finite; a program needn't handle non-finite values.
Results may differ from a plain program's by a relative error of at most 0.024.
Values may be sent and summed in bfloat16 or wider, within the bound.
A program may use at most 128 MiB of HBM per device.

v0:
```python
import jax
import jax.numpy as jnp
from jax import lax
from jax.sharding import PartitionSpec as P

D = 8192


EPS = 1e-05


def from_behind(value, axis, steps):
    count = lax.axis_size(axis)
    initial, last = (max(0, -steps), min(count, count - steps))
    return lax.ppermute(value, axis, [(source, source + steps) for source in range(initial, last)])


def on_device(tokens, norm_gain, w_gate, w_up, w_down):
    section_index = lax.axis_index("section")
    is_first = section_index == 0
    gain = norm_gain[0]
    gate_tile = w_gate[0]
    up_tile = w_up[0]
    down_tile = w_down[0]
    micro, tok_col, width_row = tokens.shape
    hidden_cols = gate_tile.shape[1]
    results = []
    received = jnp.zeros((tok_col, width_row), jnp.bfloat16)
    for tick in range(micro + 1):
        fresh = tokens[tick] if tick < micro else jnp.zeros((tok_col, width_row), jnp.bfloat16)
        block_in = jnp.where(is_first, fresh, received)
        wide_in = block_in.astype(jnp.float32)
        sum_sq = lax.psum(jnp.sum(wide_in * wide_in, axis=1), "row")
        wide = block_in.astype(jnp.float32)
        scale = lax.rsqrt(sum_sq / D + EPS)
        normed = (wide * scale[:, None] * gain[None, :]).astype(jnp.bfloat16)
        normed_rows = lax.all_gather(normed, "col", axis=0, tiled=True)
        gate_part = jnp.dot(normed_rows, gate_tile, preferred_element_type=jnp.float32)
        up_part = jnp.dot(normed_rows, up_tile, preferred_element_type=jnp.float32)
        pair = jnp.concatenate([gate_part, up_part], axis=1)
        share = lax.psum_scatter(
            pair.astype(jnp.bfloat16), "row", scatter_dimension=0, tiled=True
        ).astype(jnp.float32)
        hidden_share = (jax.nn.silu(share[:, :hidden_cols]) * share[:, hidden_cols:]).astype(
            jnp.bfloat16
        )
        hidden = lax.all_gather(hidden_share, "row", axis=0, tiled=True)
        ffn = lax.psum_scatter(
            jnp.dot(hidden, down_tile, preferred_element_type=jnp.float32).astype(jnp.bfloat16),
            "col",
            scatter_dimension=0,
            tiled=True,
        ).astype(jnp.float32)
        result = (wide_in + ffn).astype(jnp.bfloat16)
        results.append(result)
        if tick < micro:
            received = from_behind(result, "section", 1)
    early = jnp.stack(results[:micro], axis=0)
    late = jnp.stack(results[1:], axis=0)
    return jnp.where(is_first, early, late)[None]


def solution(mesh):
    placed = (
        P(None, ("group", "col"), "row"),
        P("section", "row"),
        P("section", "row", "col"),
        P("section", "row", "col"),
        P("section", "col", "row"),
    )
    return jax.shard_map(
        on_device,
        mesh=mesh,
        in_specs=placed,
        out_specs=P("section", None, ("group", "col"), "row"),
        check_vma=False,
    )
```

profile of v0, /device:TPU:1, one launch (start us, length us, event | category | flops | bytes accessed | tf_op | source)
XLA Modules:
  0.0 454.8 jit_solution(14409287867418705781)
XLA Ops:
  7.7 4.3 psum.21
  13.9 30.3 %all-gather.4.cloned.1.call-done = bf16[128,4096]{1,0:T(8,128)(2,1)} async-done(((bf16[32,4096]{1,0:T(8,128)(2,1)}), bf16[128,4096]{1,0:T(8,128)(2,1)}) %all-gather.4.cloned.1.call-update) | async-done | bytes 1048592 | tf_op jit(solution)/shard_map/all_gather | solution.py:37
  44.2 13.7 %fusion.27 = bf16[128,3584]{1,0:T(8,128)(2,1)S(1)} fusion(bf16[128,4096]{1,0:T(8,128)(2,1)} %all-gather.4.cloned.1.call-done, bf16[1,4096,3584]{2,1,0:T(8,128)(2,1)} %param.8), kind=kOutput, calls=%fused_computation.21 | convolution fusion | flops 3758555136 | bytes 31326208 | tf_op jit(solution)/shard_map/dot_general | solution.py:39
  57.9 11.6 %fusion.18 = bf16[128,3584]{1,0:T(8,128)(2,1)S(1)} fusion(bf16[128,4096]{1,0:T(8,128)(2,1)S(1)} %copy-done, bf16[1,4096,3584]{2,1,0:T(8,128)(2,1)} %param.7), kind=kOutput, calls=%fused_computation.18 | convolution fusion | flops 3758555136 | bytes 31326208 | tf_op jit(solution)/shard_map/dot_general | solution.py:38
  71.0 28.8 %reduce-scatter.7.cloned.1.call-done = bf16[64,7168]{1,0:T(8,128)(2,1)} async-done(((bf16[128,7168]{1,0:T(8,128)(2,1)}), bf16[64,7168]{1,0:T(8,128)(2,1)}) %reduce-scatter.7.cloned.1.call-update) | async-done | bytes 917520 | tf_op jit(solution)/shard_map/reduce_scatter | solution.py:41
  101.4 11.9 %all_gather.19 = bf16[128,3584]{1,0:T(8,128)(2,1)S(1)} all-gather(bf16[64,3584]{1,0:T(8,128)(2,1)S(1)} %fusion.47), channel_id=1, replica_groups=mesh['group'=2,'col'=4,'row'=2,'section'=2] {'row'}, dimensions={0}, use_global_device_ids=true | all-gather | bytes 1376256 | tf_op jit(solution)/shard_map/all_gather | solution.py:47
  113.3 12.6 %fusion.36 = bf16[128,4096]{1,0:T(8,128)(2,1)} fusion(bf16[128,3584]{1,0:T(8,128)(2,1)S(1)} %all_gather.19, bf16[1,3584,4096]{2,1,0:T(8,128)(2,1)} %param.9), kind=kOutput, calls=%fused_computation.24 | convolution fusion | flops 3758620672 | bytes 31326208 | tf_op jit(solution)/shard_map/dot_general | solution.py:49
  125.9 28.0 %reduce-scatter.9.cloned.1.call-done = bf16[32,4096]{1,0:T(8,128)(2,1)} async-done(((bf16[128,4096]{1,0:T(8,128)(2,1)}), bf16[32,4096]{1,0:T(8,128)(2,1)}) %reduce-scatter.9.cloned.1.call-update) | async-done | bytes 262160 | tf_op jit(solution)/shard_map/reduce_scatter | solution.py:48
  158.7 3.8 psum.22
  163.5 26.9 %all-gather.6.cloned.1.call-done = bf16[128,4096]{1,0:T(8,128)(2,1)} async-done(((bf16[32,4096]{1,0:T(8,128)(2,1)}), bf16[128,4096]{1,0:T(8,128)(2,1)}) %all-gather.6.cloned.1.call-update) | async-done | bytes 1048592 | tf_op jit(solution)/shard_map/all_gather | solution.py:37
  190.4 13.7 %fusion.30 = bf16[128,3584]{1,0:T(8,128)(2,1)S(1)} fusion(bf16[128,4096]{1,0:T(8,128)(2,1)} %all-gather.6.cloned.1.call-done, bf16[1,4096,3584]{2,1,0:T(8,128)(2,1)} %param.8), kind=kOutput, calls=%fused_computation.22 | convolution fusion | flops 3758555136 | bytes 31326208 | tf_op jit(solution)/shard_map/dot_general | solution.py:39
  204.2 11.6 %fusion.21 = bf16[128,3584]{1,0:T(8,128)(2,1)S(1)} fusion(bf16[128,4096]{1,0:T(8,128)(2,1)S(1)} %copy-done.1, bf16[1,4096,3584]{2,1,0:T(8,128)(2,1)} %param.7), kind=kOutput, calls=%fused_computation.19 | convolution fusion | flops 3758555136 | bytes 31326208 | tf_op jit(solution)/shard_map/dot_general | solution.py:38
  217.3 28.8 %reduce-scatter.11.cloned.1.call-done = bf16[64,7168]{1,0:T(8,128)(2,1)} async-done(((bf16[128,7168]{1,0:T(8,128)(2,1)}), bf16[64,7168]{1,0:T(8,128)(2,1)}) %reduce-scatter.11.cloned.1.call-update) | async-done | bytes 917520 | tf_op jit(solution)/shard_map/reduce_scatter | solution.py:41
  247.7 11.9 %all_gather.21 = bf16[128,3584]{1,0:T(8,128)(2,1)S(1)} all-gather(bf16[64,3584]{1,0:T(8,128)(2,1)S(1)} %fusion.46), channel_id=1, replica_groups=mesh['group'=2,'col'=4,'row'=2,'section'=2] {'row'}, dimensions={0}, use_global_device_ids=true | all-gather | bytes 1376256 | tf_op jit(solution)/shard_map/all_gather | solution.py:47
  259.5 12.5 %fusion.39 = bf16[128,4096]{1,0:T(8,128)(2,1)} fusion(bf16[128,3584]{1,0:T(8,128)(2,1)S(1)} %all_gather.21, bf16[1,3584,4096]{2,1,0:T(8,128)(2,1)} %param.9), kind=kOutput, calls=%fused_computation.25 | convolution fusion | flops 3758620672 | bytes 31326208 | tf_op jit(solution)/shard_map/dot_general | solution.py:49
  272.2 28.0 %reduce-scatter.13.cloned.1.call-done = bf16[32,4096]{1,0:T(8,128)(2,1)} async-done(((bf16[128,4096]{1,0:T(8,128)(2,1)}), bf16[32,4096]{1,0:T(8,128)(2,1)}) %reduce-scatter.13.cloned.1.call-update) | async-done | bytes 262160 | tf_op jit(solution)/shard_map/reduce_scatter | solution.py:48
  304.8 3.8 psum.23
  309.7 26.9 %all-gather.8.cloned.1.call-done = bf16[128,4096]{1,0:T(8,128)(2,1)} async-done(((bf16[32,4096]{1,0:T(8,128)(2,1)}), bf16[128,4096]{1,0:T(8,128)(2,1)}) %all-gather.8.cloned.1.call-update) | async-done | bytes 1048592 | tf_op jit(solution)/shard_map/all_gather | solution.py:37
  336.6 13.7 %fusion.33 = bf16[128,3584]{1,0:T(8,128)(2,1)S(1)} fusion(bf16[128,4096]{1,0:T(8,128)(2,1)} %all-gather.8.cloned.1.call-done, bf16[1,4096,3584]{2,1,0:T(8,128)(2,1)} %param.8), kind=kOutput, calls=%fused_computation.23 | convolution fusion | flops 3758555136 | bytes 31326208 | tf_op jit(solution)/shard_map/dot_general | solution.py:39
  350.3 11.6 %fusion.24 = bf16[128,3584]{1,0:T(8,128)(2,1)S(1)} fusion(bf16[128,4096]{1,0:T(8,128)(2,1)S(1)} %copy-done.2, bf16[1,4096,3584]{2,1,0:T(8,128)(2,1)} %param.7), kind=kOutput, calls=%fused_computation.20 | convolution fusion | flops 3758555136 | bytes 31326208 | tf_op jit(solution)/shard_map/dot_general | solution.py:38
  363.4 28.8 %reduce-scatter.15.cloned.1.call-done = bf16[64,7168]{1,0:T(8,128)(2,1)} async-done(((bf16[128,7168]{1,0:T(8,128)(2,1)}), bf16[64,7168]{1,0:T(8,128)(2,1)}) %reduce-scatter.15.cloned.1.call-update) | async-done | bytes 917520 | tf_op jit(solution)/shard_map/reduce_scatter | solution.py:41
  393.8 11.9 %all_gather.23 = bf16[128,3584]{1,0:T(8,128)(2,1)S(1)} all-gather(bf16[64,3584]{1,0:T(8,128)(2,1)S(1)} %fusion.45), channel_id=1, replica_groups=mesh['group'=2,'col'=4,'row'=2,'section'=2] {'row'}, dimensions={0}, use_global_device_ids=true | all-gather | bytes 1376256 | tf_op jit(solution)/shard_map/all_gather | solution.py:47
  405.7 12.5 %fusion.42 = bf16[128,4096]{1,0:T(8,128)(2,1)} fusion(bf16[128,3584]{1,0:T(8,128)(2,1)S(1)} %all_gather.23, bf16[1,3584,4096]{2,1,0:T(8,128)(2,1)} %param.9), kind=kOutput, calls=%fused_computation.26 | convolution fusion | flops 3758620672 | bytes 31326208 | tf_op jit(solution)/shard_map/dot_general | solution.py:49
  418.3 28.1 %reduce-scatter.17.cloned.1.call-done = bf16[32,4096]{1,0:T(8,128)(2,1)} async-done(((bf16[128,4096]{1,0:T(8,128)(2,1)}), bf16[32,4096]{1,0:T(8,128)(2,1)}) %reduce-scatter.17.cloned.1.call-update) | async-done | bytes 262160 | tf_op jit(solution)/shard_map/reduce_scatter | solution.py:48
  (54 shorter events, 25.6 us)
Async XLA Ops:
  6.5 37.6 %all-gather.4.cloned.1.call-start = ((), (), s32[]{:S(2)}) async-start(), calls=%async_computation.6 | async-start | bytes 1310720 | tf_op jit(solution)/shard_map/all_gather | solution.py:37
  13.8 86.0 %reduce-scatter.7.cloned.1.call-start = ((), (), s32[]{:S(2)}) async-start(), calls=%async_computation.7 | async-start | bytes 2752512 | tf_op jit(solution)/shard_map/reduce_scatter | solution.py:41
  44.2 13.7 %copy-start = (bf16[128,4096]{1,0:T(8,128)(2,1)S(1)}, bf16[128,4096]{1,0:T(8,128)(2,1)}, u32[]{:S(2)}) copy-start(bf16[128,4096]{1,0:T(8,128)(2,1)} %all-gather.4.cloned.1.call-done) | copy-start | bytes 3145732
  71.0 83.0 %reduce-scatter.9.cloned.1.call-start = ((), (), s32[]{:S(2)}) async-start(), calls=%async_computation.8 | async-start | bytes 1310720 | tf_op jit(solution)/shard_map/reduce_scatter | solution.py:48
  113.3 40.7 %copy-start.3 = (bf16[2,32,4096]{2,1,0:T(8,128)(2,1)S(1)}, bf16[2,32,4096]{2,1,0:T(8,128)(2,1)}, u32[]{:S(2)}) copy-start(bf16[2,32,4096]{2,1,0:T(8,128)(2,1)} %param.5) | copy-start | bytes 1572868
  113.3 49.2 %copy-start.4 = (f32[1,4096]{1,0:T(1,128)S(1)}, f32[1,4096]{1,0:T(1,128)}, u32[]{:S(2)}) copy-start(f32[1,4096]{1,0:T(1,128)} %param.6) | copy-start | bytes 49156
  125.9 64.5 %all-gather.6.cloned.1.call-start = ((), (), s32[]{:S(2)}) async-start(), calls=%async_computation.9 | async-start | bytes 1310720 | tf_op jit(solution)/shard_map/all_gather | solution.py:37
  155.0 3.4 collective-permute-start
  163.3 82.8 %reduce-scatter.11.cloned.1.call-start = ((), (), s32[]{:S(2)}) async-start(), calls=%async_computation.10 | async-start | bytes 2752512 | tf_op jit(solution)/shard_map/reduce_scatter | solution.py:41
  190.4 13.7 %copy-start.1 = (bf16[128,4096]{1,0:T(8,128)(2,1)S(1)}, bf16[128,4096]{1,0:T(8,128)(2,1)}, u32[]{:S(2)}) copy-start(bf16[128,4096]{1,0:T(8,128)(2,1)} %all-gather.6.cloned.1.call-done) | copy-start | bytes 3145732
  217.2 83.0 %reduce-scatter.13.cloned.1.call-start = ((), (), s32[]{:S(2)}) async-start(), calls=%async_computation.11 | async-start | bytes 1310720 | tf_op jit(solution)/shard_map/reduce_scatter | solution.py:48
  272.1 64.5 %all-gather.8.cloned.1.call-start = ((), (), s32[]{:S(2)}) async-start(), calls=%async_computation.12 | async-start | bytes 1310720 | tf_op jit(solution)/shard_map/all_gather | solution.py:37
  301.2 3.4 collective-permute-start.1
  309.5 82.8 %reduce-scatter.15.cloned.1.call-start = ((), (), s32[]{:S(2)}) async-start(), calls=%async_computation.13 | async-start | bytes 2752512 | tf_op jit(solution)/shard_map/reduce_scatter | solution.py:41
  336.6 13.7 %copy-start.2 = (bf16[128,4096]{1,0:T(8,128)(2,1)S(1)}, bf16[128,4096]{1,0:T(8,128)(2,1)}, u32[]{:S(2)}) copy-start(bf16[128,4096]{1,0:T(8,128)(2,1)} %all-gather.8.cloned.1.call-done) | copy-start | bytes 3145732
  363.4 83.0 %reduce-scatter.17.cloned.1.call-start = ((), (), s32[]{:S(2)}) async-start(), calls=%async_computation.14 | async-start | bytes 1310720 | tf_op jit(solution)/shard_map/reduce_scatter | solution.py:48
Sparse Core Ops, SparseCore 0:
  13.9 30.1 all-gather.3
  71.1 28.6 reduce-scatter.6
  126.0 27.9 reduce-scatter.8
  163.4 26.9 all-gather.5
  217.4 28.6 reduce-scatter.10
  272.2 27.9 reduce-scatter.12
  309.6 26.9 all-gather.7
  363.5 28.6 reduce-scatter.14
  418.4 27.9 reduce-scatter.16
where the time goes:
time: 456 us; the launch traced here: 455 us
  waiting for transfers between devices  259 us (57%)
  matrix products  114 us (25%)
  blocking collectives  47.6 us (10%)
  other arithmetic  17.9 us (4%)
  between operations  13.4 us (3%)
    reduce_scatter x3, waiting for transfers between devices, on_device(): lax.psum_scatter(pair.astype(jnp.bfloat16), 'row', scatter_dimension=0, t...  86.4 us
    reduce_scatter x3, waiting for transfers between devices, on_device(): lax.psum_scatter(jnp.dot(hidden, down_tile, preferred_element_type=jnp.fl...  84.2 us
    all_gather x3, waiting for transfers between devices, on_device(): normed_rows = lax.all_gather(normed, 'col', axis=0, tiled=True)  84 us
    dot_general x3, matrix products, on_device(): up_part = jnp.dot(normed_rows, up_tile, preferred_element_type=jnp.float32)  41.2 us
    dot_general x3, matrix products, on_device(): jnp.dot(hidden, down_tile, preferred_element_type=jnp.float32)  37.7 us
    all_gather x3, blocking collectives, on_device(): hidden = lax.all_gather(hidden_share, 'row', axis=0, tiled=True)  35.7 us
    dot_general x3, matrix products, on_device(): jnp.dot(normed_rows, gate_tile, preferred_element_type=jnp.float32)  34.8 us
    psum x3, blocking collectives, on_device(): sum_sq = lax.psum(jnp.sum(wide_in * wide_in, axis=1), 'row')  11.9 us
  transfers between devices with their start and end apart: 11, of which 11 were waited for; matrix products, arithmetic and copies ran while one was open for 0% of the time, Pallas kernels for 0%

commit v1 on v0

v1 whole, which is shorter than its diff:
```python
import functools

import jax
import jax.numpy as jnp
from jax import lax
from jax.experimental import pallas as pl
from jax.experimental.pallas import tpu as pltpu
from jax.sharding import PartitionSpec as P

EPS = 1e-05
LAG = 3
VMEM_BYTES = 67_043_328
RESERVE = 3 * 1024 * 1024
MESH = pl.DeviceIdType.MESH


def widest(size, options):
    return next(w for w in options if size % w == 0)


def kernel(
    dims,
    tok_ref, gain_ref, wg_ref, wu_ref, wd_ref, out_ref,
    wa, wb, hbuf, ss, sr, xb, gu, gr, hid, fo, fr,
    wa_sem, wb_sem, h_send, h_recv, ss_send, ss_recv, ag_send, ag_recv,
    gu_send, gu_recv, hd_send, hd_recv, fo_send, fo_recv,
):
    C, R, M, TC, DR, FC, D, F, n, S, N, nb, SB = dims
    T = TC * C
    TS = T // R
    c = lax.axis_index("col")
    r = lax.axis_index("row")
    s = lax.axis_index("section")

    def load_a(q):
        slot = lax.rem(q, S)
        cols = pl.ds(pl.multiple_of(lax.rem(q, n) * F, F), F)
        return (
            pltpu.make_async_copy(wg_ref.at[0, :, cols], wa.at[slot, 0], wa_sem.at[slot, 0]),
            pltpu.make_async_copy(wu_ref.at[0, :, cols], wa.at[slot, 1], wa_sem.at[slot, 1]),
        )

    def load_b(q):
        slot = lax.rem(q, SB)
        cols = pl.ds(pl.multiple_of(lax.rem(q, nb) * N, N), N)
        return pltpu.make_async_copy(wd_ref.at[0, :, cols], wb.at[slot], wb_sem.at[slot])

    def col_peer(d):
        return lax.rem(c + d, C)

    def row_peer(d):
        return lax.rem(r + d, R)

    def tok_rows(index):
        return pl.ds(pl.multiple_of(index * TC, TC), TC)

    def share_rows(index):
        return pl.ds(pl.multiple_of(index * TS, TS), TS)

    def ss_copy(m, d):
        return pltpu.make_async_remote_copy(
            src_ref=ss.at[m], dst_ref=sr.at[m, d - 1],
            send_sem=ss_send.at[m, d - 1], recv_sem=ss_recv.at[m, d - 1],
            device_id={"row": row_peer(d)}, device_id_type=MESH)

    def ag_copy(m, d, owner):
        return pltpu.make_async_remote_copy(
            src_ref=xb.at[m, tok_rows(owner)], dst_ref=xb.at[m, tok_rows(owner)],
            send_sem=ag_send.at[m, d - 1], recv_sem=ag_recv.at[m, d - 1],
            device_id={"col": col_peer(d)}, device_id_type=MESH)

    def gu_copy(m, i, d):
        return pltpu.make_async_remote_copy(
            src_ref=gu.at[m, i, share_rows(row_peer(d))], dst_ref=gr.at[m, i, d - 1],
            send_sem=gu_send.at[m, i, d - 1], recv_sem=gu_recv.at[m, i, d - 1],
            device_id={"row": row_peer(d)}, device_id_type=MESH)

    def hd_copy(m, i, d, owner):
        k = lax.rem(m * (n - S) + i, n)
        cols = pl.ds(pl.multiple_of(k * F, F), F)
        return pltpu.make_async_remote_copy(
            src_ref=hid.at[m, share_rows(owner), cols], dst_ref=hid.at[m, share_rows(owner), cols],
            send_sem=hd_send.at[m, i, d - 1], recv_sem=hd_recv.at[m, i, d - 1],
            device_id={"row": row_peer(d)}, device_id_type=MESH)

    def fo_copy(m, i, d):
        v = lax.rem(m * (nb - SB) + i, nb)
        cols = pl.ds(pl.multiple_of(v * N, N), N)
        return pltpu.make_async_remote_copy(
            src_ref=fo.at[m, tok_rows(col_peer(d)), cols], dst_ref=fr.at[m, d - 1, :, cols],
            send_sem=fo_send.at[m, i, d - 1], recv_sem=fo_recv.at[m, i, d - 1],
            device_id={"col": col_peer(d)}, device_id_type=MESH)

    def h_copy(m):
        return pltpu.make_async_remote_copy(
            src_ref=out_ref.at[0, m], dst_ref=hbuf.at[m],
            send_sem=h_send.at[m], recv_sem=h_recv.at[m],
            device_id={"section": 1 - s}, device_id_type=MESH)

    for q in range(S):
        for copy in load_a(q):
            copy.start()
    for q in range(SB):
        load_b(q).start()

    barrier = pltpu.get_barrier_semaphore()
    for d in range(1, C):
        pl.semaphore_signal(barrier, inc=1, device_id={"col": col_peer(d)}, device_id_type=MESH)
    for d in range(1, R):
        pl.semaphore_signal(barrier, inc=1, device_id={"row": row_peer(d)}, device_id_type=MESH)
    pl.semaphore_signal(barrier, inc=1, device_id={"section": 1 - s}, device_id_type=MESH)
    pl.semaphore_wait(barrier, C + R - 1)

    for m in range(M):
        @pl.when(s == 0)
        def _():
            hbuf[m] = tok_ref[m]

        @pl.when(s == 1)
        def _():
            h_copy(m).wait_recv()

        wide = hbuf[m].astype(jnp.float32)
        ss[m] = jnp.broadcast_to(jnp.sum(wide * wide, axis=1, keepdims=True), (TC, 128))
        for d in range(1, R):
            ss_copy(m, d).start()
        total = ss[m]
        for d in range(1, R):
            ss_copy(m, d).wait_recv()
            total = total + sr[m, d - 1]
        scale = lax.rsqrt(total[:, :1] / D + EPS)
        normed = hbuf[m].astype(jnp.float32) * scale * gain_ref[...]
        xb[m, tok_rows(c)] = normed.astype(jnp.bfloat16)
        for d in range(1, C):
            ag_copy(m, d, c).start()

    def up_step(t, carry):
        @pl.when(t < M * n)
        def _():
            m = lax.div(t, n)
            i = lax.rem(t, n)
            q = m * (n - S) + i
            slot = lax.rem(q, S)

            @pl.when(i == 0)
            def _():
                for d in range(1, C):
                    ag_copy(m, d, lax.rem(c + C - d, C)).wait_recv()

            @pl.when(jnp.logical_or(m == 0, i >= S))
            def _():
                for copy in load_a(q):
                    copy.wait()

            x = xb[m]
            for part in range(2):
                gu[m, i, :, part * F:(part + 1) * F] = jnp.dot(
                    x, wa[slot, part], preferred_element_type=jnp.float32
                ).astype(jnp.bfloat16)
            for d in range(1, R):
                gu_copy(m, i, d).start()

            @pl.when(i < n - S)
            def _():
                for copy in load_a(q + S):
                    copy.start()

        @pl.when(t >= LAG)
        def _():
            e = t - LAG
            m = lax.div(e, n)
            i = lax.rem(e, n)
            pair = gu[m, i, share_rows(r)].astype(jnp.float32)
            for d in range(1, R):
                gu_copy(m, i, d).wait_recv()
                pair = pair + gr[m, i, d - 1].astype(jnp.float32)
            gate = pair[:, :F]
            act = gate / (1.0 + jnp.exp(-gate)) * pair[:, F:]
            k = lax.rem(m * (n - S) + i, n)
            cols = pl.ds(pl.multiple_of(k * F, F), F)
            hid[m, share_rows(r), cols] = act.astype(jnp.bfloat16)
            for d in range(1, R):
                hd_copy(m, i, d, r).start()

        return carry

    lax.fori_loop(0, M * n + LAG, up_step, 0)

    def down_step(t, carry):
        m = lax.div(t, nb)
        i = lax.rem(t, nb)
        q = m * (nb - SB) + i
        slot = lax.rem(q, SB)

        @pl.when(i == 0)
        def _():
            def wait_hidden(j, inner):
                for d in range(1, R):
                    hd_copy(m, j, d, lax.rem(r + R - d, R)).wait_recv()
                return inner

            lax.fori_loop(0, n, wait_hidden, 0)

        @pl.when(jnp.logical_or(m == 0, i >= SB))
        def _():
            load_b(q).wait()

        cols = pl.ds(pl.multiple_of(lax.rem(q, nb) * N, N), N)
        fo[m, :, cols] = jnp.dot(
            hid[m], wb[slot], preferred_element_type=jnp.float32
        ).astype(jnp.bfloat16)
        for d in range(1, C):
            fo_copy(m, i, d).start()

        @pl.when(i < nb - SB)
        def _():
            load_b(q + SB).start()

        return carry

    lax.fori_loop(0, M * nb, down_step, 0)

    for m in range(M):
        def finish(i, carry):
            v = lax.rem(m * (nb - SB) + i, nb)
            cols = pl.ds(pl.multiple_of(v * N, N), N)
            ffn = fo[m, tok_rows(c), cols].astype(jnp.float32)
            for d in range(1, C):
                fo_copy(m, i, d).wait_recv()
                ffn = ffn + fr[m, d - 1, :, cols].astype(jnp.float32)
            out_ref[0, m, :, cols] = (hbuf[m, :, cols].astype(jnp.float32) + ffn).astype(jnp.bfloat16)
            return carry

        lax.fori_loop(0, nb, finish, 0)

        @pl.when(s == 0)
        def _():
            h_copy(m).start()

    for m in range(M):
        @pl.when(s == 0)
        def _():
            h_copy(m).wait_send()

        for d in range(1, R):
            ss_copy(m, d).wait_send()
        for d in range(1, C):
            ag_copy(m, d, c).wait_send()

        def drain_row(i, carry):
            for d in range(1, R):
                gu_copy(m, i, d).wait_send()
                hd_copy(m, i, d, r).wait_send()
            return carry

        lax.fori_loop(0, n, drain_row, 0)

        def drain_col(i, carry):
            for d in range(1, C):
                fo_copy(m, i, d).wait_send()
            return carry

        lax.fori_loop(0, nb, drain_col, 0)


def on_device(tokens, norm_gain, w_gate, w_up, w_down):
    C = lax.axis_size("col")
    R = lax.axis_size("row")
    M, TC, DR = tokens.shape
    FC = w_gate.shape[2]
    D = DR * R
    T = TC * C
    TS = T // R
    F = widest(FC, (256, 128))
    n = FC // F
    N = widest(DR, (512, 256, 128))
    nb = DR // N
    bf, f32 = jnp.bfloat16, jnp.float32
    acts = [
        ((M, TC, DR), bf),
        ((M, TC, 128), f32),
        ((M, R - 1, TC, 128), f32),
        ((M, T, DR), bf),
        ((M, n, T, 2 * F), bf),
        ((M, n, R - 1, TS, 2 * F), bf),
        ((M, T, FC), bf),
        ((M, T, DR), bf),
        ((M, C - 1, TC, DR), bf),
    ]

    def size(shape, dtype):
        total = jnp.dtype(dtype).itemsize
        for extent in shape:
            total *= extent
        return total

    used = sum(size(*a) for a in acts) + 2 * size((M, TC, DR), bf) + 8 * size((1, DR), f32)
    room = VMEM_BYTES - RESERVE - used
    a_bytes = size((2, DR, F), bf)
    b_bytes = size((FC, N), bf)
    SB = min(nb, max(2, (room // 3) // b_bytes))
    S = min(n, (room - SB * b_bytes) // a_bytes)
    dma = pltpu.SemaphoreType.DMA
    dims = (C, R, M, TC, DR, FC, D, F, n, S, N, nb, SB)
    vmem = pl.BlockSpec(memory_space=pltpu.VMEM)
    hbm = pl.BlockSpec(memory_space=pl.ANY)
    return pl.pallas_call(
        functools.partial(kernel, dims),
        out_shape=jax.ShapeDtypeStruct((1, M, TC, DR), bf),
        in_specs=[vmem, vmem, hbm, hbm, hbm],
        out_specs=vmem,
        scratch_shapes=[
            pltpu.VMEM((S, 2, DR, F), bf),
            pltpu.VMEM((SB, FC, N), bf),
            *[pltpu.VMEM(shape, dtype) for shape, dtype in acts],
            dma((S, 2)), dma((SB,)),
            dma((M,)), dma((M,)),
            dma((M, R - 1)), dma((M, R - 1)),
            dma((M, C - 1)), dma((M, C - 1)),
            dma((M, n, R - 1)), dma((M, n, R - 1)),
            dma((M, n, R - 1)), dma((M, n, R - 1)),
            dma((M, nb, C - 1)), dma((M, nb, C - 1)),
        ],
        compiler_params=pltpu.CompilerParams(
            collective_id=0, has_side_effects=True, vmem_limit_bytes=VMEM_BYTES
        ),
        name="two_blocks",
    )(tokens, norm_gain, w_gate, w_up, w_down)


def solution(mesh):
    placed = (
        P(None, ("group", "col"), "row"),
        P("section", "row"),
        P("section", "row", "col"),
        P("section", "row", "col"),
        P("section", "col", "row"),
    )
    return jax.shard_map(
        on_device,
        mesh=mesh,
        in_specs=placed,
        out_specs=P("section", None, ("group", "col"), "row"),
        check_vma=False,
    )
```

time: 456 us -> 158 us (0.35)
  waiting for transfers between devices: 259 us -> 0 us
  Pallas kernels: 0 us -> 156 us
  matrix products: 114 us -> 0 us
  blocking collectives: 47.6 us -> 0 us
  other arithmetic: 17.9 us -> 0 us
  between operations: 13.4 us -> 0.01 us
    reduce_scatter x6 -> x0, waiting for transfers between devices: 171 us -> none  [the longest x3 86.4 us: on_device(): lax.psum_scatter(pair.astype(jnp.bfloat16), 'row', scatter_dimension=0, t...]
    pallas_call x0 -> x1, Pallas kernels: none -> 156 us  [on_device(): pl.pallas_call(functools.partial(kernel, dims), out_shape=jax.ShapeDtypeS...]
    dot_general x9 -> x0, matrix products: 114 us -> none  [the longest x3 41.2 us: on_device(): up_part = jnp.dot(normed_rows, up_tile, preferred_element_type=jnp.float32)]
    all_gather x3 -> x0, waiting for transfers between devices: 84 us -> none  [on_device(): normed_rows = lax.all_gather(normed, 'col', axis=0, tiled=True)]
    all_gather x3 -> x0, blocking collectives: 35.7 us -> none  [on_device(): hidden = lax.all_gather(hidden_share, 'row', axis=0, tiled=True)]
    psum x3 -> x0, blocking collectives: 11.9 us -> none  [on_device(): sum_sq = lax.psum(jnp.sum(wide_in * wide_in, axis=1), 'row')]
    convert_element_type x11 -> x0, other arithmetic: 10.1 us -> none  [the longest x3 3.89 us: on_device(): share = lax.psum_scatter(pair.astype(jnp.bfloat16), 'row', scatter_dimens...]
  transfers between devices with their start and end apart: 11 -> 0, of which waited for: 11 -> 0; matrix products, arithmetic and copies ran while one was open for 0% -> 0% of each run, Pallas kernels for 0% -> 0%
where the time goes in v1:
time: 158 us
  Pallas kernels  156 us (99%)
  local copies, waits for them, and re-layouts  1.87 us (1%)
    pallas_call x1, Pallas kernels, on_device(): pl.pallas_call(functools.partial(kernel, dims), out_shape=jax.ShapeDtypeS...  156 us

profile of v1, /device:TPU:1, one launch (start us, length us, event | category | flops | bytes accessed | tf_op | source)
XLA Modules:
  0.0 158.2 jit_solution(18057152171811230560)
XLA Ops:
  0.0 156.3 %two_blocks.1 = bf16[1,2,32,4096]{3,2,1,0:T(8,128)(2,1)} custom-call(bf16[2,32,4096]{2,1,0:T(8,128)(2,1)} %tok_ref.1, f32[1,4096]{1,0:T(1,128)} %gain_ref.1, bf16[1,4096,3584]{2,1,0:T(8,128)(2,1)} %wg_ref.1, bf16[1,4096,3584]{2,1,0:T(8,128)(2,1)} %wu_ref.1, bf16[1,3584,4096]{2,1,0:T(8,128)(2,1)} %wd_ref.1), custom_call_target="tpu_custom_call" | custom-call | tf_op jit(solution)/shard_map/two_blocks/pallas_call | solution.py:307
  156.3 1.9 %copy.7 = bf16[1,2,32,4096]{3,2,1,0:T(8,128)(2,1)} copy(bf16[1,2,32,4096]{3,2,1,0:T(8,128)(2,1)} %two_blocks.1) | data formatting | bytes 1048576

commit v2 on v1

--- a/solution.py
+++ b/solution.py
@@ -9,6 +9,7 @@
 
 EPS = 1e-05
 LAG = 3
+LATE = 5
 VMEM_BYTES = 67_043_328
 RESERVE = 3 * 1024 * 1024
 MESH = pl.DeviceIdType.MESH
@@ -28,6 +29,7 @@
     C, R, M, TC, DR, FC, D, F, n, S, N, nb, SB = dims
     T = TC * C
     TS = T // R
+    CLOSE = min(LATE, n + LAG - 1)
     c = lax.axis_index("col")
     r = lax.axis_index("row")
     s = lax.axis_index("section")
@@ -111,7 +113,7 @@
     pl.semaphore_signal(barrier, inc=1, device_id={"section": 1 - s}, device_id_type=MESH)
     pl.semaphore_wait(barrier, C + R - 1)
 
-    for m in range(M):
+    def norm(m):
         @pl.when(s == 0)
         def _():
             hbuf[m] = tok_ref[m]
@@ -134,11 +136,27 @@
         for d in range(1, C):
             ag_copy(m, d, c).start()
 
-    def up_step(t, carry):
-        @pl.when(t < M * n)
-        def _():
-            m = lax.div(t, n)
-            i = lax.rem(t, n)
+    def close(m):
+        def finish(i, carry):
+            v = lax.rem(m * (nb - SB) + i, nb)
+            cols = pl.ds(pl.multiple_of(v * N, N), N)
+            ffn = fo[m, tok_rows(c), cols].astype(jnp.float32)
+            for d in range(1, C):
+                fo_copy(m, i, d).wait_recv()
+                ffn = ffn + fr[m, d - 1, :, cols].astype(jnp.float32)
+            out_ref[0, m, :, cols] = (hbuf[m, :, cols].astype(jnp.float32) + ffn).astype(jnp.bfloat16)
+            return carry
+
+        lax.fori_loop(0, nb, finish, 0)
+
+        @pl.when(s == 0)
+        def _():
+            h_copy(m).start()
+
+    def up_step(m, t, carry):
+        @pl.when(t < n)
+        def _():
+            i = t
             q = m * (n - S) + i
             slot = lax.rem(q, S)
 
@@ -147,7 +165,7 @@
                 for d in range(1, C):
                     ag_copy(m, d, lax.rem(c + C - d, C)).wait_recv()
 
-            @pl.when(jnp.logical_or(m == 0, i >= S))
+            @pl.when(i >= 0 if m == 0 else i >= S)
             def _():
                 for copy in load_a(q):
                     copy.wait()
@@ -167,9 +185,7 @@
 
         @pl.when(t >= LAG)
         def _():
-            e = t - LAG
-            m = lax.div(e, n)
-            i = lax.rem(e, n)
+            i = t - LAG
             pair = gu[m, i, share_rows(r)].astype(jnp.float32)
             for d in range(1, R):
                 gu_copy(m, i, d).wait_recv()
@@ -182,13 +198,14 @@
             for d in range(1, R):
                 hd_copy(m, i, d, r).start()
 
+        if m > 0:
+            @pl.when(t == CLOSE)
+            def _():
+                close(m - 1)
+
         return carry
 
-    lax.fori_loop(0, M * n + LAG, up_step, 0)
-
-    def down_step(t, carry):
-        m = lax.div(t, nb)
-        i = lax.rem(t, nb)
+    def down_step(m, i, carry):
         q = m * (nb - SB) + i
         slot = lax.rem(q, SB)
 
@@ -201,7 +218,7 @@
 
             lax.fori_loop(0, n, wait_hidden, 0)
 
-        @pl.when(jnp.logical_or(m == 0, i >= SB))
+        @pl.when(i >= 0 if m == 0 else i >= SB)
         def _():
             load_b(q).wait()
 
@@ -218,24 +235,23 @@
 
         return carry
 
-    lax.fori_loop(0, M * nb, down_step, 0)
 
     for m in range(M):
-        def finish(i, carry):
-            v = lax.rem(m * (nb - SB) + i, nb)
-            cols = pl.ds(pl.multiple_of(v * N, N), N)
-            ffn = fo[m, tok_rows(c), cols].astype(jnp.float32)
-            for d in range(1, C):
-                fo_copy(m, i, d).wait_recv()
-                ffn = ffn + fr[m, d - 1, :, cols].astype(jnp.float32)
-            out_ref[0, m, :, cols] = (hbuf[m, :, cols].astype(jnp.float32) + ffn).astype(jnp.bfloat16)
-            return carry
-
-        lax.fori_loop(0, nb, finish, 0)
-
-        @pl.when(s == 0)
-        def _():
-            h_copy(m).start()
+        if m == 0:
+            norm(0)
+
+            @pl.when(s == 0)
+            def _():
+                for later in range(1, M):
+                    norm(later)
+        else:
+            @pl.when(s == 1)
+            def _():
+                norm(m)
+
+        lax.fori_loop(0, n + LAG, functools.partial(up_step, m), 0)
+        lax.fori_loop(0, nb, functools.partial(down_step, m), 0)
+    close(M - 1)
 
     for m in range(M):
         @pl.when(s == 0)

time: 158 us -> 156 us (0.987)
  Pallas kernels: 156 us -> 154 us
    pallas_call x1, Pallas kernels: 156 us -> 154 us  [on_device(): pl.pallas_call(functools.partial(kernel, dims), out_shape=jax.ShapeDtypeS...]
where the time goes in v2:
time: 156 us
  Pallas kernels  154 us (99%)
  local copies, waits for them, and re-layouts  1.87 us (1%)
    pallas_call x1, Pallas kernels, on_device(): pl.pallas_call(functools.partial(kernel, dims), out_shape=jax.ShapeDtypeS...  154 us

profile of v2, /device:TPU:1, one launch (start us, length us, event | category | flops | bytes accessed | tf_op | source)
XLA Modules:
  0.0 155.6 jit_solution(4482539962795022603)
XLA Ops:
  0.0 153.7 %two_blocks.1 = bf16[1,2,32,4096]{3,2,1,0:T(8,128)(2,1)} custom-call(bf16[2,32,4096]{2,1,0:T(8,128)(2,1)} %tok_ref.1, f32[1,4096]{1,0:T(1,128)} %gain_ref.1, bf16[1,4096,3584]{2,1,0:T(8,128)(2,1)} %wg_ref.1, bf16[1,4096,3584]{2,1,0:T(8,128)(2,1)} %wu_ref.1, bf16[1,3584,4096]{2,1,0:T(8,128)(2,1)} %wd_ref.1), custom_call_target="tpu_custom_call" | custom-call | tf_op jit(solution)/shard_map/two_blocks/pallas_call | solution.py:323
  153.7 1.9 %copy.7 = bf16[1,2,32,4096]{3,2,1,0:T(8,128)(2,1)} copy(bf16[1,2,32,4096]{3,2,1,0:T(8,128)(2,1)} %two_blocks.1) | data formatting | bytes 1048576
